TPU v7x, 128 devices: a whole 4x4x4 slice. The times are simulated.
128 devices in a mesh: dp: 64 (over z, y, x_hi, core), tensor: 2 (over x_lo).
Axes of the slice: x: 4 (x_hi: 2, x_lo: 2; x = x_hi * 2 + x_lo), y: 4, z: 4, core: 2. Of those that a mesh axis runs over, the one named last changes fastest.
Arguments:
- tokens: bfloat16 [65536, 2048], P('dp', 'tensor'), may hold values from -30 to 30
- norm_gain: bfloat16 [2048], P('tensor'), may hold values from 0.5 to 7
- w_query: bfloat16 [2048, 2048], P(None, 'tensor'), may hold values from -0.125 to 0.125
- key_weight: bfloat16 [2048, 1024], P(None, 'tensor'), may hold values from -0.125 to 0.125
- value_weight: bfloat16 [2048, 1024], P(None, 'tensor'), may hold values from -0.125 to 0.125
- w_out: bfloat16 [2048, 2048], P('tensor'), may hold values from -0.125 to 0.125
- valid_lengths: int32 [64], P('dp'), may hold values from 1 to 1024, as said below
- earlier_cache_pages: bfloat16 [4096, 2, 8, 32, 128], P('dp', None, 'tensor'), may hold values from -6 to 6
- page_owner: int32 [4096], P('dp'), may hold values from 0 to 63, as said below
- page_slot: int32 [4096], P('dp'), may hold values from 0 to 63, as said below
- page_live: int32 [4096], P('dp'), may hold values 0 or 1
Outputs:
- mixed: bfloat16 [65536, 2048], P('dp', 'tensor')
- decode_pages: bfloat16 [8, 4096, 2, 32, 128], P('tensor', 'dp')
Inputs may be any that keep to these rules, and one draw needn't show every extreme that they name: `valid_lengths`: some request has all 1024 tokens valid. `page_owner`: the 64 pages of each source dp index name every dp index exactly once. `page_slot`: pages that name the same owner carry different slots.
All inputs are finite; a program needn't handle non-finite values. No bound on the sum of `page_live` on one device may be relied on, other than what follows from the above.
Results may differ from a plain program's by a relative error of at most 0.01065.
The roundings to bfloat16 on the way count: a program that leaves them out, or rounds other values in their place, can miss the bound.
Values may be sent and summed in bfloat16 or wider, within the bound.
A program may use at most 192 MiB of HBM per device.

v0:
```python
import jax
import jax.numpy as jnp
from jax import lax
from jax.sharding import PartitionSpec as P

MODEL_WIDTH = 2048
HEAD_SIZE = 128


NORM_EPS = 1e-05
ROPE_THETA = 1000000.0


def rotary_tables(values, token_positions):
    dim = values.shape[-1]
    half = dim // 2
    freqs = ROPE_THETA ** (-jnp.arange(half, dtype=jnp.float32) * 2.0 / dim)
    angles = token_positions.astype(jnp.float32)[:, None] * freqs[None, :]
    cosine = jnp.cos(angles)[:, None, :]
    sine = jnp.sin(angles)[:, None, :]
    first = values[..., :half]
    second = values[..., half:]
    return jnp.concatenate(
        [first * cosine - second * sine, second * cosine + first * sine], axis=-1
    )


def project_inputs(tokens, norm_gain, w_query, key_weight, value_weight):
    values = tokens.astype(jnp.float32)
    row_total = lax.psum(jnp.sum(values * values, axis=-1), "tensor")
    row_scale = lax.rsqrt(row_total / MODEL_WIDTH + NORM_EPS)
    normed = (values * row_scale[:, None] * norm_gain.astype(jnp.float32)).astype(jnp.bfloat16)
    shard_part = lax.all_gather(normed, "tensor", axis=1, tiled=True)
    return (
        jnp.dot(shard_part, w_query, preferred_element_type=jnp.float32),
        jnp.dot(shard_part, key_weight, preferred_element_type=jnp.float32),
        jnp.dot(shard_part, value_weight, preferred_element_type=jnp.float32),
    )


def prefill_layer(tokens, norm_gain, w_query, key_weight, value_weight, w_out, valid_lengths):
    query_raw, key_unrotated, value_projected = project_inputs(
        tokens, norm_gain, w_query, key_weight, value_weight
    )
    token_count = tokens.shape[0]
    heads_query = w_query.shape[1] // HEAD_SIZE
    heads_kv = key_weight.shape[1] // HEAD_SIZE
    token_positions = jnp.arange(token_count)
    query_vectors = rotary_tables(
        query_raw.reshape(token_count, heads_query, HEAD_SIZE), token_positions
    ).astype(jnp.bfloat16)
    query_vectors = query_vectors.reshape(token_count, heads_kv, heads_query // heads_kv, HEAD_SIZE)
    key_turned = rotary_tables(
        key_unrotated.reshape(token_count, heads_kv, HEAD_SIZE), token_positions
    ).astype(jnp.bfloat16)
    value_halfprec = value_projected.reshape(token_count, heads_kv, HEAD_SIZE).astype(jnp.bfloat16)
    length = valid_lengths[0]
    block_rows = min(512, token_count)
    outputs = []
    for block_index in range(token_count // block_rows):
        first_row = block_index * block_rows
        query_block = query_vectors[first_row : first_row + block_rows]
        scores = jnp.einsum(
            "qgrd,kgd->grqk", query_block, key_turned, preferred_element_type=jnp.float32
        ) * HEAD_SIZE ** (-0.5)
        query_pos = first_row + jnp.arange(block_rows)
        key_pos = jnp.arange(token_count)
        allowed = (key_pos[None, :] <= query_pos[:, None]) & (key_pos[None, :] < length)
        scores = jnp.where(allowed, scores, -1e30)
        row_peak = jnp.max(scores, axis=-1, keepdims=True)
        exponent = jnp.exp(scores - row_peak)
        attn_weights = (exponent / jnp.sum(exponent, axis=-1, keepdims=True)).astype(jnp.bfloat16)
        block_out = jnp.einsum(
            "grqk,kgd->qgrd", attn_weights, value_halfprec, preferred_element_type=jnp.float32
        )
        outputs.append(block_out.astype(jnp.bfloat16).reshape(block_rows, heads_query * HEAD_SIZE))
    attended = jnp.concatenate(outputs, axis=0)
    summed = lax.psum_scatter(
        lax.dot_general(
            w_out, attended, (((0,), (1,)), ((), ())), preferred_element_type=jnp.float32
        ).astype(jnp.bfloat16),
        "tensor",
        scatter_dimension=0,
        tiled=True,
    ).astype(jnp.float32)
    return (tokens.astype(jnp.float32) + summed.T).astype(jnp.bfloat16)


def move_pages(earlier_cache_pages, page_owner, page_slot, page_live):
    peer_count = lax.axis_size("dp")
    slot_count = earlier_cache_pages.shape[0]
    outgoing = (
        jnp.zeros((peer_count,) + earlier_cache_pages.shape[1:], jnp.bfloat16)
        .at[page_owner]
        .set(earlier_cache_pages)
    )
    labels = jnp.where(page_live == 1, page_slot, -1)
    slot_tags = jnp.full((peer_count,), -1, jnp.int32).at[page_owner].set(labels)
    incoming, in_tags = (
        lax.all_to_all(outgoing, "dp", split_axis=0, concat_axis=0, tiled=True),
        lax.all_to_all(slot_tags, "dp", split_axis=0, concat_axis=0, tiled=True),
    )
    target = jnp.where(in_tags >= 0, in_tags, slot_count).astype(jnp.int32)
    owner_placed = jnp.zeros_like(earlier_cache_pages).at[target].set(incoming, mode="drop")
    return jnp.transpose(owner_placed, (2, 0, 1, 3, 4))


def on_device(
    tokens,
    norm_gain,
    w_query,
    key_weight,
    value_weight,
    w_out,
    valid_lengths,
    earlier_cache_pages,
    page_owner,
    page_slot,
    page_live,
):
    mixed = prefill_layer(
        tokens, norm_gain, w_query, key_weight, value_weight, w_out, valid_lengths
    )
    decode_pages = move_pages(earlier_cache_pages, page_owner, page_slot, page_live)
    return (mixed, decode_pages)


def solution(mesh):
    return jax.shard_map(
        on_device,
        mesh=mesh,
        in_specs=(
            P("dp", "tensor"),
            P("tensor"),
            P(None, "tensor"),
            P(None, "tensor"),
            P(None, "tensor"),
            P("tensor", None),
            P("dp"),
            P("dp", None, "tensor", None, None),
            P("dp"),
            P("dp"),
            P("dp"),
        ),
        out_specs=(P("dp", "tensor"), P("tensor", "dp", None, None, None)),
        check_vma=False,
    )
```

profile of v0, /device:TPU:1, one launch (start us, length us, event | category | flops | bytes accessed | tf_op | source)
XLA Modules:
  0.0 288.6 jit_solution(228853129367546269)
XLA Ops:
  8.1 2.1 fusion.12
  10.1 4.4 %psum.7 = f32[1024]{0:T(1024)S(1)} all-reduce(f32[1024]{0:T(1024)S(1)} %fusion.12), channel_id=1, replica_groups=mesh['dp'=64,'tensor'=2] {'tensor'}, use_global_device_ids=true, to_apply=%region_1.0 | all-reduce | flops 1024 | bytes 8192 | tf_op jit(solution)/shard_map/psum | solution.py:30
  14.5 3.5 %fusion.14 = bf16[1024,1024]{1,0:T(8,128)(2,1)} fusion(bf16[1024,1024]{1,0:T(8,128)(2,1)} %param.11, f32[1024]{0:T(1024)S(1)} %convert_element_type.69, f32[1024]{0:T(1024)S(1)} %add_rsqrt_fusion), kind=kLoop, calls=%fused_computation.26 | loop fusion | flops 4194304 | bytes 4202496 | tf_op jit(solution)/shard_map/convert_element_type | solution.py:32
  19.7 1.0 copy.55
  20.7 1.0 copy.53
  21.7 1.6 fusion.19
  23.2 57.9 %all-gather.2.cloned.1.call-done = bf16[1024,2048]{1,0:T(8,128)(2,1)} async-done(((bf16[1024,1024]{1,0:T(8,128)(2,1)}), bf16[1024,2048]{1,0:T(8,128)(2,1)}) %all-gather.2.cloned.1.call-update) | async-done | bytes 4194320 | tf_op jit(solution)/shard_map/all_gather | solution.py:33
  81.2 7.6 %fusion.40 = f32[1024,1024]{0,1:T(8,128)S(1)} fusion(bf16[1024,2048]{1,0:T(8,128)(2,1)} %all-gather.2.cloned.1.call-done, bf16[2048,1024]{1,0:T(8,128)(2,1)} %param.13), kind=kOutput, calls=%fused_computation.73 | convolution fusion | flops 4294967296 | bytes 12582912 | tf_op jit(solution)/shard_map/dot_general | solution.py:35
  88.8 2.1 subtract_convert_fusion
  91.7 2.4 fusion.39
  94.2 1.2 fusion.36
  95.3 1.8 copy.67
  97.2 1.9 copy.66
  99.1 3.2 %fusion.27 = (bf16[512,8,128]{0,2,1:T(8,128)(2,1)}, bf16[512,8,128]{0,2,1:T(8,128)(2,1)}) fusion(bf16[1024,8,64]{0,2,1:T(8,128)(2,1)} %get-tuple-element.12, bf16[1024,8,64]{0,2,1:T(8,128)(2,1)} %get-tuple-element.13), kind=kLoop, calls=%fused_computation.47 | loop fusion | flops 4194304 | bytes 4194304 | tf_op jit(solution)/shard_map/concatenate | solution.py:23
  102.3 1.5 subtract_convert_fusion.1
  103.9 11.3 %fusion.37 = (f32[4,2,512]{2,1,0:T(2,128)S(1)}, f32[4,2,512,1024]{2,3,1,0:T(8,128)}) fusion(pred[512,1024]{0,1:T(8,128)(4,1)} %get-tuple-element.21, bf16[512,4,2,128]{0,3,2,1:T(8,128)(2,1)} %bitcast.78, bf16[1024,4,64]{2,0,1:T(8,128)(2,1)} %get-tuple-element.11, bf16[1024,4,64]{2,0,1:T(8,128)(2,1)S(1)} %get-tuple-element.10), kind=kOutput, calls=%fused_computation.70 | convolution fusion | flops 1092617216 | bytes 19415040 | tf_op jit(solution)/shard_map/sub | solution.py:71
  115.2 10.7 %fusion.38 = (f32[4,2,512]{2,1,0:T(2,128)S(1)}, f32[4,2,512,1024]{2,3,1,0:T(8,128)}) fusion(pred[512,1024]{0,1:T(8,128)(4,1)} %get-tuple-element.20, bf16[512,4,2,128]{0,3,2,1:T(8,128)(2,1)S(1)} %bitcast.77, bf16[1024,4,64]{2,0,1:T(8,128)(2,1)S(1)} %copy-done.5, bf16[1024,4,64]{2,0,1:T(8,128)(2,1)S(1)} %get-tuple-element.10), kind=kOutput, calls=%fused_computation.71 | convolution fusion | flops 1092617216 | bytes 19415040 | tf_op jit(solution)/shard_map/sub | solution.py:71
  125.9 5.4 %convolution_convert_fusion = bf16[1024,512]{0,1:T(8,128)(2,1)S(1)} fusion(bf16[1024,2048]{1,0:T(8,128)(2,1)} %all-gather.2.cloned.1.call-done, bf16[2048,512]{1,0:T(8,128)(2,1)} %param.15), kind=kOutput, calls=%fused_computation.46 | convolution fusion | flops 2148007936 | bytes 7340032 | tf_op jit(solution)/shard_map/dot_general | solution.py:37
  131.2 2.2 copy-done.12
  133.5 1.5 fusion.25
  135.0 7.2 %fusion.26 = bf16[4,128,2,512]{3,1,2,0:T(8,128)(2,1)S(1)} fusion(bf16[1024,4,128,1]{0,2,3,1:T(8,128)(2,1)S(1)} %bitcast.81, f32[4,2,512,1024]{2,3,1,0:T(8,128)} %get-tuple-element.25, f32[4,2,512]{2,1,0:T(2,128)S(1)} %get-tuple-element.24), kind=kOutput, calls=%fused_computation.45 | convolution fusion | flops 1082654720 | bytes 18890752 | tf_op jit(solution)/shard_map/grqk,kgd->qgrd/dot_general | solution.py:73
  142.2 6.2 %convert_bitcast_fusion = bf16[2048,1024]{0,1:T(8,128)(2,1)} fusion(bf16[1024,2048]{1,0:T(8,128)(2,1)S(1)} %copy-done.10, bf16[512,1024]{0,1:T(8,128)(2,1)S(1)} %bitcast.82, bf16[512,1024]{0,1:T(8,128)(2,1)S(1)} %bitcast.83), kind=kOutput, calls=%fused_computation.28 | convolution fusion | flops 4301258752 | bytes 10485760 | tf_op jit(solution)/shard_map/dot_general | solution.py:79
  150.6 10.2 %all-to-all-start = ((s32[64,1,1]{2,1,0:T(1,128)}), s32[64,1,1]{2,1,0:T(1,128)S(1)}, u32[]{:S(2)}, u32[]{:S(2)}) async-start(s32[64,1,1]{2,1,0:T(1,128)} %copy.60), calls=%async_computation.1 | async-start | bytes 65536 | tf_op jit(solution)/shard_map/all_to_all | solution.py:101
  160.9 3.1 %broadcast.111.clone = bf16[64,2,4,32,128]{4,3,2,1,0:T(8,128)(2,1)} broadcast(bf16[]{:T(256)} %constant.9.clone.1), dimensions={} | broadcast | bytes 4194306 | tf_op jit(solution)/shard_map/broadcast.9
  163.9 11.9 %scatter_fusion = bf16[64,2,4,32,128]{4,3,2,1,0:T(8,128)(2,1)} fusion(bf16[64,2,4,32,128]{4,3,2,1,0:T(8,128)(2,1)} %broadcast.111.clone, s32[64]{0:T(128)S(1)} %get-tuple-element.26, bf16[64,2,4,32,128]{4,3,2,1,0:T(8,128)(2,1)} %param.18), kind=kCustom, calls=%fused_computation.1 | custom fusion | bytes 12583168 | tf_op jit(solution)/shard_map/scatter | solution.py:95
  175.9 10.8 %all-to-all-start.1 = ((bf16[64,2,4,32,128]{4,3,2,1,0:T(8,128)(2,1)}), bf16[64,2,4,32,128]{4,3,2,1,0:T(8,128)(2,1)}, u32[]{:S(2)}, u32[]{:S(2)}) async-start(bf16[64,2,4,32,128]{4,3,2,1,0:T(8,128)(2,1)} %scatter_fusion), calls=%async_computation.2 | async-start | bytes 8388608 | tf_op jit(solution)/shard_map/all_to_all | solution.py:100
  186.6 1.2 reduce
  187.9 68.8 %all-to-all-done.1 = bf16[64,2,4,32,128]{4,3,2,1,0:T(8,128)(2,1)} async-done(((bf16[64,2,4,32,128]{4,3,2,1,0:T(8,128)(2,1)}), bf16[64,2,4,32,128]{4,3,2,1,0:T(8,128)(2,1)}, u32[]{:S(2)}, u32[]{:S(2)}) %all-to-all-start.1) | async-done | bytes 4194336 | tf_op jit(solution)/shard_map/all_to_all | solution.py:100
  256.7 3.0 %broadcast.111 = bf16[64,2,4,32,128]{4,3,2,1,0:T(8,128)(2,1)} broadcast(bf16[]{:T(256)} %constant.9.clone.1), dimensions={} | broadcast | bytes 4194306 | tf_op jit(solution)/shard_map/broadcast.9
  259.7 12.0 %scatter_fusion.1 = bf16[64,2,4,32,128]{4,3,2,1,0:T(8,128)(2,1)} fusion(bf16[64,2,4,32,128]{4,3,2,1,0:T(8,128)(2,1)} %broadcast.111, s32[64]{0:T(128)S(1)} %fusion.28, bf16[64,2,4,32,128]{4,3,2,1,0:T(8,128)(2,1)} %all-to-all-done.1), kind=kCustom, calls=%fused_computation.2 | custom fusion | bytes 12583168 | tf_op jit(solution)/shard_map/scatter | solution.py:104
  271.6 5.6 %copy.61 = bf16[4,64,2,32,128]{4,3,2,1,0:T(8,128)(2,1)} copy(bf16[4,64,2,32,128]{4,3,0,2,1:T(8,128)(2,1)} %bitcast.74) | data formatting | bytes 8388608
  277.3 4.5 %fusion.15 = bf16[1024,1024]{1,0:T(8,128)(2,1)} fusion(bf16[1024,1024]{1,0:T(8,128)(2,1)} %param.11, bf16[1024,1024]{0,1:T(8,128)(2,1)} %reduce-scatter.2.cloned.1.call-done), kind=kLoop, calls=%fused_computation.27 | loop fusion | flops 4194304 | bytes 6291456 | tf_op jit(solution)/shard_map/convert_element_type | solution.py:86
  (42 shorter events, 5.0 us)
Async XLA Ops:
  7.2 83.7 %copy-start = (bf16[2048,512]{1,0:T(8,128)(2,1)S(1)}, bf16[2048,512]{1,0:T(8,128)(2,1)}, u32[]{:S(2)}) copy-start(bf16[2048,512]{1,0:T(8,128)(2,1)} %param.14) | copy-start | bytes 6291460
  7.2 74.0 %all-gather.2.cloned.1.call-start = ((), (), s32[]{:S(2)}) async-start(), calls=%async_computation.3 | async-start | bytes 6291456 | tf_op jit(solution)/shard_map/all_gather | solution.py:33
  18.0 259.3 %reduce-scatter.2.cloned.1.call-start = ((), (), s32[]{:S(2)}) async-start(), calls=%async_computation.4 | async-start | bytes 6291456 | tf_op jit(solution)/shard_map/reduce_scatter | solution.py:78
  88.8 2.9 %copy-start.11 = (bf16[1024,2048]{1,0:T(8,128)(2,1)S(1)}, bf16[1024,2048]{1,0:T(8,128)(2,1)}, u32[]{:S(2)}) copy-start(bf16[1024,2048]{1,0:T(8,128)(2,1)} %all-gather.2.cloned.1.call-done) | copy-start | bytes 12582916
  99.1 3.2 %copy-start.2 = (f32[1024,4,64]{2,0,1:T(8,128)S(1)}, f32[1024,4,64]{2,0,1:T(8,128)}, u32[]{:S(2)}) copy-start(f32[1024,4,64]{2,0,1:T(8,128)} %copy.66) | copy-start | bytes 3145732
  99.1 3.2 %copy-start.3 = (f32[1024,64]{1,0:T(8,128)S(1)}, f32[1024,64]{1,0:T(8,128)}, u32[]{:S(2)}) copy-start(f32[1024,64]{1,0:T(8,128)} %copy.55) | copy-start | bytes 786436
  99.1 3.2 %copy-start.4 = (f32[1024,64]{1,0:T(8,128)S(1)}, f32[1024,64]{1,0:T(8,128)}, u32[]{:S(2)}) copy-start(f32[1024,64]{1,0:T(8,128)} %copy.53) | copy-start | bytes 786436
  103.8 11.3 %copy-start.5 = (bf16[1024,4,64]{2,0,1:T(8,128)(2,1)S(1)}, bf16[1024,4,64]{2,0,1:T(8,128)(2,1)}, u32[]{:S(2)}) copy-start(bf16[1024,4,64]{2,0,1:T(8,128)(2,1)} %get-tuple-element.11) | copy-start | bytes 1572868
  103.8 11.3 %copy-start.6 = (bf16[512,8,128]{0,2,1:T(8,128)(2,1)S(1)}, bf16[512,8,128]{0,2,1:T(8,128)(2,1)}, u32[]{:S(2)}) copy-start(bf16[512,8,128]{0,2,1:T(8,128)(2,1)} %get-tuple-element.14) | copy-start | bytes 3145732
  125.9 7.6 %copy-start.12 = (f32[4,2,512,1024]{2,3,1,0:T(8,128)S(1)}, f32[4,2,512,1024]{2,3,1,0:T(8,128)}, u32[]{:S(2)}) copy-start(f32[4,2,512,1024]{2,3,1,0:T(8,128)} %get-tuple-element.23) | copy-start | bytes 50331652
  135.0 7.2 %copy-start.10 = (bf16[1024,2048]{1,0:T(8,128)(2,1)S(1)}, bf16[1024,2048]{1,0:T(8,128)(2,1)}, u32[]{:S(2)}) copy-start(bf16[1024,2048]{1,0:T(8,128)(2,1)} %param.16) | copy-start | bytes 12582916
  148.5 0.7 copy-start.7
  148.5 0.7 copy-start.8
  148.5 0.7 copy-start.9
  150.6 25.2 %all-to-all-start = ((s32[64,1,1]{2,1,0:T(1,128)}), s32[64,1,1]{2,1,0:T(1,128)S(1)}, u32[]{:S(2)}, u32[]{:S(2)}) async-start(s32[64,1,1]{2,1,0:T(1,128)} %copy.60), calls=%async_computation.1 | async-start | bytes 65536 | tf_op jit(solution)/shard_map/all_to_all | solution.py:101
  175.9 80.8 %all-to-all-start.1 = ((bf16[64,2,4,32,128]{4,3,2,1,0:T(8,128)(2,1)}), bf16[64,2,4,32,128]{4,3,2,1,0:T(8,128)(2,1)}, u32[]{:S(2)}, u32[]{:S(2)}) async-start(bf16[64,2,4,32,128]{4,3,2,1,0:T(8,128)(2,1)} %scatter_fusion), calls=%async_computation.2 | async-start | bytes 8388608 | tf_op jit(solution)/shard_map/all_to_all | solution.py:100
  271.6 10.2 %copy-start.1 = (bf16[2048,512]{1,0:T(8,128)(2,1)S(1)}, bf16[2048,512]{1,0:T(8,128)(2,1)}, u32[]{:S(2)}) copy-start(bf16[2048,512]{1,0:T(8,128)(2,1)} %param.14) | copy-start | bytes 6291460
Sparse Core Ops, SparseCore 0:
  18.1 63.0 all-gather.1
  148.6 75.8 reduce-scatter.1
where the time goes:
time: 289 us
  waiting for transfers between devices  127 us (44%)
  matrix products  52.3 us (18%)
  local copies, waits for them, and re-layouts  47.8 us (17%)
  other arithmetic  21.4 us (7%)
  starting transfers between devices  21.1 us (7%)
  between operations  14.9 us (5%)
  blocking collectives  4.36 us (2%)
    all_to_all x1, waiting for transfers between devices, move_pages(): lax.all_to_all(outgoing, 'dp', split_axis=0, concat_axis=0, tiled=True)  68.8 us
    all_gather x1, waiting for transfers between devices, project_inputs(): shard_part = lax.all_gather(normed, 'tensor', axis=1, tiled=True)  57.9 us
    sub x2, matrix products, prefill_layer(): exponent = jnp.exp(scores - row_peak)  22 us
    unnamed x29, local copies, waits for them, and re-layouts  13.2 us
    scatter x1, local copies, waits for them, and re-layouts, move_pages(): jnp.zeros_like(earlier_cache_pages).at[target].set(incoming, mode='drop')  12 us
    scatter x1, local copies, waits for them, and re-layouts, move_pages(): outgoing = jnp.zeros((peer_count,) + earlier_cache_pages.shape[1:], jnp.b...  11.9 us
    all_to_all x1, starting transfers between devices, move_pages(): lax.all_to_all(outgoing, 'dp', split_axis=0, concat_axis=0, tiled=True)  10.8 us
    all_to_all x1, starting transfers between devices, move_pages(): lax.all_to_all(slot_tags, 'dp', split_axis=0, concat_axis=0, tiled=True)  10.2 us
  transfers between devices with their start and end apart: 4, of which 2 were waited for; matrix products, arithmetic and copies ran while one was open for 15% of the time, Pallas kernels for 0%

commit v1 on v0

--- a/solution.py
+++ b/solution.py
@@ -26,15 +26,17 @@
 
 
 def project_inputs(tokens, norm_gain, w_query, key_weight, value_weight):
-    values = tokens.astype(jnp.float32)
-    row_total = lax.psum(jnp.sum(values * values, axis=-1), "tensor")
-    row_scale = lax.rsqrt(row_total / MODEL_WIDTH + NORM_EPS)
-    normed = (values * row_scale[:, None] * norm_gain.astype(jnp.float32)).astype(jnp.bfloat16)
-    shard_part = lax.all_gather(normed, "tensor", axis=1, tiled=True)
+    full_rows = lax.all_gather(tokens, "tensor", axis=1, tiled=True)
+    full_gain = lax.all_gather(norm_gain, "tensor", axis=0, tiled=True)
+    values = full_rows.astype(jnp.float32)
+    mean_sq = jnp.mean(values * values, axis=-1, keepdims=True)
+    normed = (values * lax.rsqrt(mean_sq + NORM_EPS) * full_gain.astype(jnp.float32)).astype(
+        jnp.bfloat16
+    )
     return (
-        jnp.dot(shard_part, w_query, preferred_element_type=jnp.float32),
-        jnp.dot(shard_part, key_weight, preferred_element_type=jnp.float32),
-        jnp.dot(shard_part, value_weight, preferred_element_type=jnp.float32),
+        jnp.dot(normed, w_query, preferred_element_type=jnp.float32),
+        jnp.dot(normed, key_weight, preferred_element_type=jnp.float32),
+        jnp.dot(normed, value_weight, preferred_element_type=jnp.float32),
     )
 
 
@@ -89,20 +91,23 @@
 def move_pages(earlier_cache_pages, page_owner, page_slot, page_live):
     peer_count = lax.axis_size("dp")
     slot_count = earlier_cache_pages.shape[0]
-    outgoing = (
-        jnp.zeros((peer_count,) + earlier_cache_pages.shape[1:], jnp.bfloat16)
-        .at[page_owner]
-        .set(earlier_cache_pages)
+    order = jnp.arange(slot_count, dtype=jnp.int32)
+    page_for_owner = jnp.zeros((peer_count,), jnp.int32).at[page_owner].set(order)
+    outgoing = jnp.take(earlier_cache_pages, page_for_owner, axis=0)
+    labels = jnp.where(page_live == 1, page_slot, -1)
+    slot_tags = jnp.take(labels, page_for_owner, axis=0)
+    incoming = lax.all_to_all(outgoing, "dp", split_axis=0, concat_axis=0, tiled=True)
+    in_tags = lax.all_to_all(slot_tags, "dp", split_axis=0, concat_axis=0, tiled=True)
+    target = jnp.where(in_tags >= 0, in_tags, slot_count).astype(jnp.int32)
+    source_of = (
+        jnp.full((slot_count + 1,), peer_count, jnp.int32).at[target].set(
+            jnp.arange(peer_count, dtype=jnp.int32)
+        )[:slot_count]
     )
-    labels = jnp.where(page_live == 1, page_slot, -1)
-    slot_tags = jnp.full((peer_count,), -1, jnp.int32).at[page_owner].set(labels)
-    incoming, in_tags = (
-        lax.all_to_all(outgoing, "dp", split_axis=0, concat_axis=0, tiled=True),
-        lax.all_to_all(slot_tags, "dp", split_axis=0, concat_axis=0, tiled=True),
-    )
-    target = jnp.where(in_tags >= 0, in_tags, slot_count).astype(jnp.int32)
-    owner_placed = jnp.zeros_like(earlier_cache_pages).at[target].set(incoming, mode="drop")
-    return jnp.transpose(owner_placed, (2, 0, 1, 3, 4))
+    filled = source_of < peer_count
+    heads_first = jnp.transpose(incoming, (2, 0, 1, 3, 4))
+    placed = jnp.take(heads_first, jnp.minimum(source_of, peer_count - 1), axis=1)
+    return jnp.where(filled[None, :, None, None, None], placed, jnp.zeros_like(placed))
 
 
 def on_device(

time: 289 us -> 278 us (0.962)
  local copies, waits for them, and re-layouts: 47.8 us -> 32.1 us
  other arithmetic: 21.4 us -> 25.8 us
    scatter x3 -> x2, local copies, waits for them, and re-layouts: 24.6 us -> 1.55 us  [the longest x1 0.77 us: move_pages(): jnp.full((slot_count + 1,), peer_count, jnp.int32).at[target]]
    gather x0 -> x3, local copies, waits for them, and re-layouts: none -> 11.3 us  [the longest x1 5.29 us: move_pages(): outgoing = jnp.take(earlier_cache_pages, page_for_owner, axis=0)]
    select_n x2 -> x7, other arithmetic: 0.01 us -> 7.48 us  [the longest x1 4.79 us: move_pages(): outgoing = jnp.take(earlier_cache_pages, page_for_owner, axis=0)]
    another operation x2 -> x0, local copies, waits for them, and re-layouts: 6.06 us -> none
    transpose x0 -> x1, local copies, waits for them, and re-layouts: none -> 5.49 us  [move_pages(): heads_first = jnp.transpose(incoming, (2, 0, 1, 3, 4))]
    psum x1 -> x0, blocking collectives: 4.36 us -> none  [project_inputs(): row_total = lax.psum(jnp.sum(values * values, axis=-1), 'tensor')]
    convert_element_type x2 -> x1, other arithmetic: 4.28 us -> 0.01 us  [project_inputs(): full_gain.astype(jnp.float32)]
    all_gather x0 -> x1, blocking collectives: none -> 3.95 us  [project_inputs(): full_gain = lax.all_gather(norm_gain, 'tensor', axis=0, tiled=True)]
  transfers between devices with their start and end apart: 4 -> 4, of which waited for: 2 -> 2; matrix products, arithmetic and copies ran while one was open for 15% -> 13% of each run, Pallas kernels for 0% -> 0%
where the time goes in v1:
time: 278 us; the launch traced here: 277 us
  waiting for transfers between devices  128 us (46%)
  matrix products  51.5 us (19%)
  local copies, waits for them, and re-layouts  32.1 us (12%)
  other arithmetic  25.8 us (9%)
  starting transfers between devices  20.9 us (8%)
  between operations  14.9 us (5%)
  blocking collectives  3.95 us (1%)
    all_to_all x1, waiting for transfers between devices, move_pages(): lax.all_to_all(outgoing, 'dp', split_axis=0, concat_axis=0, tiled=True)  72.3 us
    all_gather x1, waiting for transfers between devices, project_inputs(): full_rows = lax.all_gather(tokens, 'tensor', axis=1, tiled=True)  55 us
    sub x2, matrix products, prefill_layer(): exponent = jnp.exp(scores - row_peak)  22 us
    all_to_all x1, starting transfers between devices, move_pages(): lax.all_to_all(outgoing, 'dp', split_axis=0, concat_axis=0, tiled=True)  10.6 us
    all_to_all x1, starting transfers between devices, move_pages(): lax.all_to_all(slot_tags, 'dp', split_axis=0, concat_axis=0, tiled=True)  10.2 us
    unnamed x29, local copies, waits for them, and re-layouts  9.81 us
    dot_general x2, matrix products, prefill_layer(): jnp.einsum('grqk,kgd->qgrd', attn_weights, value_halfprec, preferred_elem...  8.7 us
    dot_general x1, matrix products, project_inputs(): jnp.dot(normed, w_query, preferred_element_type=jnp.float32)  6.61 us
  transfers between devices with their start and end apart: 4, of which 2 were waited for; matrix products, arithmetic and copies ran while one was open for 13% of the time, Pallas kernels for 0%

profile of v1, /device:TPU:1, one launch (start us, length us, event | category | flops | bytes accessed | tf_op | source)
XLA Modules:
  0.0 277.1 jit_solution(2306829098577122852)
XLA Ops:
  8.0 3.9 %all_gather.7 = bf16[2048]{0:T(1024)(128)(2,1)S(1)} all-gather(bf16[1024]{0:T(1024)(128)(2,1)} %param.12), channel_id=1, replica_groups=mesh['dp'=64,'tensor'=2] {'tensor'}, dimensions={0}, use_global_device_ids=true | all-gather | bytes 6144 | tf_op jit(solution)/shard_map/all_gather | solution.py:30
  13.6 1.0 copy.65
  14.6 1.0 copy.63
  15.6 1.6 fusion.19
  17.2 55.0 %all-gather.2.cloned.1.call-done = bf16[1024,2048]{1,0:T(8,128)(2,1)} async-done(((bf16[1024,1024]{1,0:T(8,128)(2,1)}), bf16[1024,2048]{1,0:T(8,128)(2,1)}) %all-gather.2.cloned.1.call-update) | async-done | bytes 4194320 | tf_op jit(solution)/shard_map/all_gather | solution.py:29
  72.2 3.2 %fusion.4 = f32[1024]{0:T(1024)S(1)} fusion(bf16[1024,2048]{1,0:T(8,128)(2,1)} %all-gather.2.cloned.1.call-done), kind=kLoop, calls=%fused_computation.17 | loop fusion | flops 6290432 | bytes 4198400 | tf_op jit(solution)/shard_map/reduce_sum | solution.py:32
  75.6 6.6 %fusion.38 = f32[1024,1024]{0,1:T(8,128)S(1)} fusion(bf16[2048,1024]{1,0:T(8,128)(2,1)} %param.13, bf16[1024,2048]{1,0:T(8,128)(2,1)S(1)} %copy-done.3, f32[2048]{0:T(1024)S(1)} %convert_element_type.72, f32[1024]{0:T(1024)S(1)} %add_rsqrt_fusion), kind=kOutput, calls=%fused_computation.83 | convolution fusion | flops 4303355904 | bytes 12595200 | tf_op jit(solution)/shard_map/dot_general | solution.py:37
  82.2 2.0 subtract_convert_fusion
  84.3 2.5 fusion.40
  86.8 1.2 fusion.43
  87.9 1.8 copy.78
  89.8 1.9 copy.77
  91.7 3.2 %fusion.27 = (bf16[512,8,128]{0,2,1:T(8,128)(2,1)}, bf16[512,8,128]{0,2,1:T(8,128)(2,1)}) fusion(bf16[1024,8,64]{0,2,1:T(8,128)(2,1)} %get-tuple-element.18, bf16[1024,8,64]{0,2,1:T(8,128)(2,1)} %get-tuple-element.19), kind=kLoop, calls=%fused_computation.51 | loop fusion | flops 4194304 | bytes 4194304 | tf_op jit(solution)/shard_map/concatenate | solution.py:23
  94.9 1.5 subtract_convert_fusion.1
  96.4 11.3 %fusion.44 = (f32[4,2,512]{2,1,0:T(2,128)S(1)}, f32[4,2,512,1024]{2,3,1,0:T(8,128)}) fusion(pred[512,1024]{0,1:T(8,128)(4,1)} %get-tuple-element.27, bf16[512,4,2,128]{0,3,2,1:T(8,128)(2,1)} %bitcast.79, bf16[1024,4,64]{2,0,1:T(8,128)(2,1)} %get-tuple-element.17, bf16[1024,4,64]{2,0,1:T(8,128)(2,1)S(1)} %get-tuple-element.16), kind=kOutput, calls=%fused_computation.86 | convolution fusion | flops 1092617216 | bytes 19415040 | tf_op jit(solution)/shard_map/sub | solution.py:73
  107.8 10.7 %fusion.45 = (f32[4,2,512]{2,1,0:T(2,128)S(1)}, f32[4,2,512,1024]{2,3,1,0:T(8,128)}) fusion(pred[512,1024]{0,1:T(8,128)(4,1)} %get-tuple-element.26, bf16[512,4,2,128]{0,3,2,1:T(8,128)(2,1)S(1)} %bitcast.78, bf16[1024,4,64]{2,0,1:T(8,128)(2,1)S(1)} %copy-done.6, bf16[1024,4,64]{2,0,1:T(8,128)(2,1)S(1)} %get-tuple-element.16), kind=kOutput, calls=%fused_computation.87 | convolution fusion | flops 1092617216 | bytes 19415040 | tf_op jit(solution)/shard_map/sub | solution.py:73
  118.5 5.5 %convolution_convert_fusion = bf16[1024,512]{0,1:T(8,128)(2,1)S(1)} fusion(bf16[2048,512]{1,0:T(8,128)(2,1)} %param.15, bf16[1024,2048]{1,0:T(8,128)(2,1)} %all-gather.2.cloned.1.call-done, f32[2048]{0:T(1024)S(1)} %convert_element_type.72, f32[1024]{0:T(1024)S(1)} %add_rsqrt_fusion), kind=kOutput, calls=%fused_computation.50 | convolution fusion | flops 2156396544 | bytes 7352320 | tf_op jit(solution)/shard_map/dot_general | solution.py:39
  124.0 2.1 copy-done.12
  126.1 1.5 fusion.25
  127.6 7.2 %fusion.26 = bf16[4,128,2,512]{3,1,2,0:T(8,128)(2,1)S(1)} fusion(bf16[1024,4,128,1]{0,2,3,1:T(8,128)(2,1)S(1)} %bitcast.81, f32[4,2,512,1024]{2,3,1,0:T(8,128)} %get-tuple-element.32, f32[4,2,512]{2,1,0:T(2,128)S(1)} %get-tuple-element.31), kind=kOutput, calls=%fused_computation.49 | convolution fusion | flops 1082654720 | bytes 18890752 | tf_op jit(solution)/shard_map/grqk,kgd->qgrd/dot_general | solution.py:75
  134.9 6.2 %convert_bitcast_fusion = bf16[2048,1024]{0,1:T(8,128)(2,1)} fusion(bf16[1024,2048]{1,0:T(8,128)(2,1)S(1)} %copy-done.8, bf16[512,1024]{0,1:T(8,128)(2,1)S(1)} %bitcast.82, bf16[512,1024]{0,1:T(8,128)(2,1)S(1)} %bitcast.83), kind=kOutput, calls=%fused_computation.31 | convolution fusion | flops 4301258752 | bytes 10485760 | tf_op jit(solution)/shard_map/dot_general | solution.py:81
  144.1 10.2 %all-to-all-start = ((s32[64,1,1]{2,1,0:T(1,128)}), s32[64,1,1]{2,1,0:T(1,128)S(1)}, u32[]{:S(2)}, u32[]{:S(2)}) async-start(s32[64,1,1]{2,1,0:T(1,128)} %copy.70), calls=%async_computation.1 | async-start | bytes 65536 | tf_op jit(solution)/shard_map/all_to_all | solution.py:100
  154.4 5.3 %gather_fusion.1 = bf16[64,2,4,32,128]{4,3,2,1,0:T(8,128)(2,1)} fusion(bf16[64,2,4,32,128]{4,3,2,1,0:T(8,128)(2,1)} %param.18, s32[1024]{0:T(1024)S(1)} %pad_clamp_fusion.1), kind=kCustom, calls=%fused_computation.1 | custom fusion | bytes 8388864 | tf_op jit(solution)/shard_map/jit(_take)/gather | solution.py:96
  159.6 4.8 %broadcast_select_fusion = bf16[64,2,4,32,128]{4,3,2,1,0:T(8,128)(2,1)} fusion(bf16[64,2,4,32,128]{4,3,2,1,0:T(8,128)(2,1)} %gather_fusion.1, pred[64]{0:T(512)(128)(4,1)S(1)} %get-tuple-element.15), kind=kLoop, calls=%fused_computation.32 | loop fusion | flops 2097152 | bytes 8388672 | tf_op jit(solution)/shard_map/jit(_take)/select_n | solution.py:96
  164.4 10.6 %all-to-all-start.1 = ((bf16[64,2,4,32,128]{4,3,2,1,0:T(8,128)(2,1)}), bf16[64,2,4,32,128]{4,3,2,1,0:T(8,128)(2,1)}, u32[]{:S(2)}, u32[]{:S(2)}) async-start(bf16[64,2,4,32,128]{4,3,2,1,0:T(8,128)(2,1)} %broadcast_select_fusion), calls=%async_computation.2 | async-start | bytes 8388608 | tf_op jit(solution)/shard_map/all_to_all | solution.py:99
  175.0 1.2 reduce
  177.1 72.3 %all-to-all-done.1 = bf16[64,2,4,32,128]{4,3,2,1,0:T(8,128)(2,1)} async-done(((bf16[64,2,4,32,128]{4,3,2,1,0:T(8,128)(2,1)}), bf16[64,2,4,32,128]{4,3,2,1,0:T(8,128)(2,1)}, u32[]{:S(2)}, u32[]{:S(2)}) %all-to-all-start.1) | async-done | bytes 4194336 | tf_op jit(solution)/shard_map/all_to_all | solution.py:99
  249.3 5.5 %copy.71 = bf16[4,64,2,32,128]{4,3,2,1,0:T(8,128)(2,1)} copy(bf16[4,64,2,32,128]{4,3,0,2,1:T(8,128)(2,1)} %bitcast.23) | data formatting | bytes 8388608 | tf_op jit(solution)/shard_map/transpose | solution.py:108
  254.8 5.3 %gather_fusion.2 = bf16[64,4,2,32,128]{4,3,2,1,0:T(8,128)(2,1)} fusion(bf16[4,64,2,32,128]{4,3,2,1,0:T(8,128)(2,1)} %copy.71, s32[1024]{0:T(1024)S(1)} %pad_clamp_fusion), kind=kCustom, calls=%fused_computation.2 | custom fusion | bytes 8388864 | tf_op jit(solution)/shard_map/jit(_take)/gather | solution.py:109
  260.1 2.7 select_bitcast_fusion
  262.8 3.0 %copy.72 = bf16[4,64,2,32,128]{4,3,2,1,0:T(8,128)(2,1)} copy(bf16[4,64,2,32,128]{4,3,2,0,1:T(8,128)(2,1)S(1)} %select_bitcast_fusion) | data formatting | bytes 8388608
  265.8 4.5 %fusion.15 = bf16[1024,1024]{1,0:T(8,128)(2,1)} fusion(bf16[1024,1024]{0,1:T(8,128)(2,1)} %reduce-scatter.2.cloned.1.call-done, bf16[1024,1024]{1,0:T(8,128)(2,1)} %param.11), kind=kLoop, calls=%fused_computation.29 | loop fusion | flops 4194304 | bytes 6291456 | tf_op jit(solution)/shard_map/convert_element_type | solution.py:88
  (52 shorter events, 5.8 us)
Async XLA Ops:
  7.2 77.1 %copy-start = (bf16[2048,512]{1,0:T(8,128)(2,1)S(1)}, bf16[2048,512]{1,0:T(8,128)(2,1)}, u32[]{:S(2)}) copy-start(bf16[2048,512]{1,0:T(8,128)(2,1)} %param.14) | copy-start | bytes 6291460
  7.2 65.0 %all-gather.2.cloned.1.call-start = ((), (), s32[]{:S(2)}) async-start(), calls=%async_computation.3 | async-start | bytes 6291456 | tf_op jit(solution)/shard_map/all_gather | solution.py:29
  7.9 257.9 %reduce-scatter.2.cloned.1.call-start = ((), (), s32[]{:S(2)}) async-start(), calls=%async_computation.4 | async-start | bytes 6291456 | tf_op jit(solution)/shard_map/reduce_scatter | solution.py:80
  72.2 3.4 %copy-start.3 = (bf16[1024,2048]{1,0:T(8,128)(2,1)S(1)}, bf16[1024,2048]{1,0:T(8,128)(2,1)}, u32[]{:S(2)}) copy-start(bf16[1024,2048]{1,0:T(8,128)(2,1)} %all-gather.2.cloned.1.call-done) | copy-start | bytes 12582916
  91.7 3.2 %copy-start.2 = (f32[1024,4,64]{2,0,1:T(8,128)S(1)}, f32[1024,4,64]{2,0,1:T(8,128)}, u32[]{:S(2)}) copy-start(f32[1024,4,64]{2,0,1:T(8,128)} %copy.77) | copy-start | bytes 3145732
  91.7 3.2 %copy-start.4 = (f32[1024,64]{1,0:T(8,128)S(1)}, f32[1024,64]{1,0:T(8,128)}, u32[]{:S(2)}) copy-start(f32[1024,64]{1,0:T(8,128)} %copy.65) | copy-start | bytes 786436
  91.7 3.2 %copy-start.5 = (f32[1024,64]{1,0:T(8,128)S(1)}, f32[1024,64]{1,0:T(8,128)}, u32[]{:S(2)}) copy-start(f32[1024,64]{1,0:T(8,128)} %copy.63) | copy-start | bytes 786436
  96.4 11.3 %copy-start.6 = (bf16[1024,4,64]{2,0,1:T(8,128)(2,1)S(1)}, bf16[1024,4,64]{2,0,1:T(8,128)(2,1)}, u32[]{:S(2)}) copy-start(bf16[1024,4,64]{2,0,1:T(8,128)(2,1)} %get-tuple-element.17) | copy-start | bytes 1572868
  96.4 11.3 %copy-start.7 = (bf16[512,8,128]{0,2,1:T(8,128)(2,1)S(1)}, bf16[512,8,128]{0,2,1:T(8,128)(2,1)}, u32[]{:S(2)}) copy-start(bf16[512,8,128]{0,2,1:T(8,128)(2,1)} %get-tuple-element.20) | copy-start | bytes 3145732
  118.5 7.6 %copy-start.12 = (f32[4,2,512,1024]{2,3,1,0:T(8,128)S(1)}, f32[4,2,512,1024]{2,3,1,0:T(8,128)}, u32[]{:S(2)}) copy-start(f32[4,2,512,1024]{2,3,1,0:T(8,128)} %get-tuple-element.30) | copy-start | bytes 50331652
  127.6 7.2 %copy-start.8 = (bf16[1024,2048]{1,0:T(8,128)(2,1)S(1)}, bf16[1024,2048]{1,0:T(8,128)(2,1)}, u32[]{:S(2)}) copy-start(bf16[1024,2048]{1,0:T(8,128)(2,1)} %param.16) | copy-start | bytes 12582916
  141.1 0.7 copy-start.9
  141.1 1.5 copy-start.10
  141.1 1.5 copy-start.11
  144.1 20.3 %all-to-all-start = ((s32[64,1,1]{2,1,0:T(1,128)}), s32[64,1,1]{2,1,0:T(1,128)S(1)}, u32[]{:S(2)}, u32[]{:S(2)}) async-start(s32[64,1,1]{2,1,0:T(1,128)} %copy.70), calls=%async_computation.1 | async-start | bytes 65536 | tf_op jit(solution)/shard_map/all_to_all | solution.py:100
  164.4 84.9 %all-to-all-start.1 = ((bf16[64,2,4,32,128]{4,3,2,1,0:T(8,128)(2,1)}), bf16[64,2,4,32,128]{4,3,2,1,0:T(8,128)(2,1)}, u32[]{:S(2)}, u32[]{:S(2)}) async-start(bf16[64,2,4,32,128]{4,3,2,1,0:T(8,128)(2,1)} %broadcast_select_fusion), calls=%async_computation.2 | async-start | bytes 8388608 | tf_op jit(solution)/shard_map/all_to_all | solution.py:99
  262.7 7.5 %copy-start.1 = (bf16[2048,512]{1,0:T(8,128)(2,1)S(1)}, bf16[2048,512]{1,0:T(8,128)(2,1)}, u32[]{:S(2)}) copy-start(bf16[2048,512]{1,0:T(8,128)(2,1)} %param.14) | copy-start | bytes 6291460
Sparse Core Ops, SparseCore 0:
  9.7 62.4 all-gather.1
  141.3 80.2 reduce-scatter.1

commit v2 on v1

v2 whole, which is shorter than its diff:
```python
import jax
import jax.numpy as jnp
from jax import lax
from jax.sharding import PartitionSpec as P
from jax.experimental import pallas as pl
from jax.experimental.pallas import tpu as pltpu
import functools

MODEL_WIDTH = 2048
HEAD_SIZE = 128


NORM_EPS = 1e-05
ROPE_THETA = 1000000.0


def rotary_tables(values, token_positions):
    dim = values.shape[-1]
    half = dim // 2
    freqs = ROPE_THETA ** (-jnp.arange(half, dtype=jnp.float32) * 2.0 / dim)
    angles = token_positions.astype(jnp.float32)[:, None] * freqs[None, :]
    cosine = jnp.cos(angles)[:, None, :]
    sine = jnp.sin(angles)[:, None, :]
    first = values[..., :half]
    second = values[..., half:]
    return jnp.concatenate(
        [first * cosine - second * sine, second * cosine + first * sine], axis=-1
    )


def project_inputs(tokens, norm_gain, w_query, key_weight, value_weight, held):
    half_width = tokens.shape[1]
    my_offset = lax.axis_index("tensor") * half_width
    other_offset = (1 - lax.axis_index("tensor")) * half_width
    swap = [(0, 1), (1, 0)]
    other_rows = lax.ppermute(tokens, "tensor", perm=swap)
    other_gain = lax.ppermute(norm_gain, "tensor", perm=swap)
    full_rows = jnp.zeros((tokens.shape[0], 2 * half_width), tokens.dtype)
    full_rows = lax.dynamic_update_slice_in_dim(full_rows, tokens, my_offset, axis=1)
    full_rows = lax.dynamic_update_slice_in_dim(full_rows, other_rows, other_offset, axis=1)
    full_gain = jnp.zeros((2 * half_width,), norm_gain.dtype)
    full_gain = lax.dynamic_update_slice_in_dim(full_gain, norm_gain, my_offset, axis=0)
    full_gain = lax.dynamic_update_slice_in_dim(full_gain, other_gain, other_offset, axis=0)
    values = full_rows.astype(jnp.float32)
    mean_sq = jnp.mean(values * values, axis=-1, keepdims=True)
    normed = (values * lax.rsqrt(mean_sq + NORM_EPS) * full_gain.astype(jnp.float32)).astype(
        jnp.bfloat16
    )
    projected = (
        jnp.dot(normed, w_query, preferred_element_type=jnp.float32),
        jnp.dot(normed, key_weight, preferred_element_type=jnp.float32),
        jnp.dot(normed, value_weight, preferred_element_type=jnp.float32),
    )
    return lax.optimization_barrier((projected, held))


def prefill_layer(tokens, norm_gain, w_query, key_weight, value_weight, w_out, valid_lengths, held, stage_two):
    (query_raw, key_unrotated, value_projected), held = project_inputs(
        tokens, norm_gain, w_query, key_weight, value_weight, held
    )
    moved = stage_two(held)
    token_count = tokens.shape[0]
    heads_query = w_query.shape[1] // HEAD_SIZE
    heads_kv = key_weight.shape[1] // HEAD_SIZE
    token_positions = jnp.arange(token_count)
    query_vectors = rotary_tables(
        query_raw.reshape(token_count, heads_query, HEAD_SIZE), token_positions
    ).astype(jnp.bfloat16)
    query_vectors = query_vectors.reshape(token_count, heads_kv, heads_query // heads_kv, HEAD_SIZE)
    key_turned = rotary_tables(
        key_unrotated.reshape(token_count, heads_kv, HEAD_SIZE), token_positions
    ).astype(jnp.bfloat16)
    value_halfprec = value_projected.reshape(token_count, heads_kv, HEAD_SIZE).astype(jnp.bfloat16)
    length = valid_lengths[0]
    block_rows = min(512, token_count)
    half_width = w_out.shape[1] // 2
    my_rows = lax.axis_index("tensor") * half_width
    other_rows = (1 - lax.axis_index("tensor")) * half_width
    outputs = []
    for block_index in range(token_count // block_rows):
        first_row = block_index * block_rows
        query_block = query_vectors[first_row : first_row + block_rows]
        key_count = first_row + block_rows
        scores = jnp.einsum(
            "qgrd,kgd->grqk", query_block, key_turned[:key_count],
            preferred_element_type=jnp.float32,
        ) * HEAD_SIZE ** (-0.5)
        query_pos = first_row + jnp.arange(block_rows)
        key_pos = jnp.arange(key_count)
        allowed = (key_pos[None, :] <= query_pos[:, None]) & (key_pos[None, :] < length)
        scores = jnp.where(allowed, scores, -1e30)
        row_peak = jnp.max(scores, axis=-1, keepdims=True)
        exponent = jnp.exp(scores - row_peak)
        attn_weights = (exponent / jnp.sum(exponent, axis=-1, keepdims=True)).astype(jnp.bfloat16)
        block_out = jnp.einsum(
            "grqk,kgd->qgrd", attn_weights, value_halfprec[:key_count],
            preferred_element_type=jnp.float32,
        )
        block_attended = block_out.astype(jnp.bfloat16).reshape(block_rows, heads_query * HEAD_SIZE)
        partial_value = lax.dot_general(
            w_out, block_attended, (((0,), (1,)), ((), ())),
            preferred_element_type=jnp.float32,
        ).astype(jnp.bfloat16)
        own_part = lax.dynamic_slice_in_dim(partial_value, my_rows, half_width, axis=0)
        sent_part = lax.dynamic_slice_in_dim(partial_value, other_rows, half_width, axis=0)
        got_part = lax.ppermute(sent_part, "tensor", perm=[(0, 1), (1, 0)])
        outputs.append(own_part.astype(jnp.float32) + got_part.astype(jnp.float32))
    summed = jnp.concatenate(outputs, axis=1)
    return (tokens.astype(jnp.float32) + summed.T).astype(jnp.bfloat16), moved


def place_kernel(source_ref, keep_ref, recv_ref, out_ref):
    slots = out_ref.shape[1]
    pairs = recv_ref.shape[1]
    heads = recv_ref.shape[2]

    def body(slot, carry):
        source = source_ref[slot]
        keep = keep_ref[slot] > 0
        for pair in range(pairs):
            for head in range(heads):
                block = recv_ref[source, pair, head]
                out_ref[head, slot, pair] = jnp.where(keep, block, jnp.zeros_like(block))
        return carry

    lax.fori_loop(0, slots, body, 0)


def place(incoming, source_of, keep):
    count, pairs, heads, rows, lanes = incoming.shape
    return pl.pallas_call(
        place_kernel,
        out_shape=jax.ShapeDtypeStruct((heads, count, pairs, rows, lanes), incoming.dtype),
        in_specs=[
            pl.BlockSpec(memory_space=pltpu.SMEM),
            pl.BlockSpec(memory_space=pltpu.SMEM),
            pl.BlockSpec(memory_space=pltpu.VMEM),
        ],
        out_specs=pl.BlockSpec(memory_space=pltpu.VMEM),
        cost_estimate=pl.CostEstimate(
            flops=0, bytes_accessed=2 * incoming.size * incoming.dtype.itemsize, transcendentals=0
        ),
    )(source_of, keep, incoming)


def move_pages(earlier_cache_pages, page_owner, page_slot, page_live):
    peer_count = lax.axis_size("dp")
    slot_count = earlier_cache_pages.shape[0]
    inner = 4
    outer = peer_count // inner
    me = lax.axis_index("dp")
    me_in = me % inner
    me_out = me // inner
    order = jnp.arange(slot_count, dtype=jnp.int32)
    page_for_owner = jnp.zeros((peer_count,), jnp.int32).at[page_owner].set(order)
    outgoing = jnp.take(earlier_cache_pages, page_for_owner, axis=0, mode="clip")
    labels = jnp.where(page_live == 1, page_slot, -1)
    slot_tags = jnp.take(labels, page_for_owner, axis=0, mode="clip")
    page_shape = outgoing.shape[1:]
    by_owner = outgoing.reshape((outer, inner) + page_shape)
    first = [lax.dynamic_index_in_dim(by_owner, me_in, axis=1, keepdims=False)]
    for shift in range(1, inner):
        target_in = (me_in + shift) % inner
        sent = lax.dynamic_index_in_dim(by_owner, target_in, axis=1, keepdims=False)
        pairs = [(d, (d // inner) * inner + (d % inner + shift) % inner) for d in range(peer_count)]
        first.append(lax.ppermute(sent, "dp", perm=pairs))
    first = jnp.stack(first, axis=0)
    return first, outgoing.shape, slot_tags


def move_pages_second(first, page_shape):
    peer_count = first.shape[0] * first.shape[1]
    inner = first.shape[0]
    outer = first.shape[1]
    me = lax.axis_index("dp")
    me_in = me % inner
    me_out = me // inner
    second = [lax.dynamic_index_in_dim(first, me_out, axis=1, keepdims=False)]
    for shift in range(1, outer):
        target_out = (me_out + shift) % outer
        sent = lax.dynamic_index_in_dim(first, target_out, axis=1, keepdims=False)
        pairs = [(d, ((d // inner + shift) % outer) * inner + d % inner) for d in range(peer_count)]
        second.append(lax.ppermute(sent, "dp", perm=pairs))
    incoming = jnp.stack(second, axis=0).reshape((peer_count,) + page_shape[1:])
    return incoming


def tags_at_positions(slot_tags):
    peer_count = slot_tags.shape[0]
    inner = 4
    outer = peer_count // inner
    me = lax.axis_index("dp")
    me_in = me % inner
    me_out = me // inner
    tag_table = lax.all_gather(slot_tags, "dp", axis=0, tiled=False)
    position = jnp.arange(peer_count, dtype=jnp.int32)
    source = ((me_out - position // inner) % outer) * inner + (me_in - position % inner) % inner
    my_column = lax.dynamic_index_in_dim(tag_table, me, axis=1, keepdims=False)
    return jnp.take(my_column, source, axis=0, mode="clip")


def place_pages(incoming, in_tags):
    peer_count = incoming.shape[0]
    slot_count = incoming.shape[0]
    target = jnp.where(in_tags >= 0, in_tags, slot_count).astype(jnp.int32)
    source_of = (
        jnp.full((slot_count + 1,), peer_count, jnp.int32).at[target].set(
            jnp.arange(peer_count, dtype=jnp.int32)
        )[:slot_count]
    )
    keep = (source_of < peer_count).astype(jnp.int32)
    return place(incoming, jnp.minimum(source_of, peer_count - 1), keep)


def on_device(
    tokens,
    norm_gain,
    w_query,
    key_weight,
    value_weight,
    w_out,
    valid_lengths,
    earlier_cache_pages,
    page_owner,
    page_slot,
    page_live,
):
    first, page_shape, slot_tags = move_pages(
        earlier_cache_pages, page_owner, page_slot, page_live
    )
    mixed, incoming = prefill_layer(
        tokens, norm_gain, w_query, key_weight, value_weight, w_out, valid_lengths,
        first, lambda held: move_pages_second(held, page_shape),
    )
    decode_pages = place_pages(incoming, tags_at_positions(slot_tags))
    return (mixed, decode_pages)


def solution(mesh):
    return jax.shard_map(
        on_device,
        mesh=mesh,
        in_specs=(
            P("dp", "tensor"),
            P("tensor"),
            P(None, "tensor"),
            P(None, "tensor"),
            P(None, "tensor"),
            P("tensor", None),
            P("dp"),
            P("dp", None, "tensor", None, None),
            P("dp"),
            P("dp"),
            P("dp"),
        ),
        out_specs=(P("dp", "tensor"), P("tensor", "dp", None, None, None)),
        check_vma=False,
    )
```

time: 278 us -> 645 us (2.32)
  the two profiles are of different devices: /device:TPU:1 before, /device:TPU:54 now
where the time goes in v2:
time: 645 us; the launch traced here: 638 us
  blocking collectives  338 us (52%)
  waiting for transfers between devices  92.6 us (14%)
  local copies, waits for them, and re-layouts  61.4 us (10%)
  starting transfers between devices  60.2 us (9%)
  matrix products  55.9 us (9%)
  other arithmetic  21.5 us (3%)
    unnamed x1, blocking collectives  338 us
    ppermute x15, waiting for transfers between devices, move_pages_second(): second.append(lax.ppermute(sent, 'dp', perm=pairs))  61.2 us
    ppermute x15, starting transfers between devices, move_pages_second(): second.append(lax.ppermute(sent, 'dp', perm=pairs))  55 us
    ppermute x2, waiting for transfers between devices, prefill_layer(): got_part = lax.ppermute(sent_part, 'tensor', perm=[(0, 1), (1, 0)])  31.4 us
    unnamed x79, local copies, waits for them, and re-layouts  21.7 us
    sub x2, matrix products, prefill_layer(): exponent = jnp.exp(scores - row_peak)  20 us
  transfers between devices with their start and end apart: 22, of which 10 were waited for; matrix products, arithmetic and copies ran while one was open for 14% of the time, Pallas kernels for 1%

profile of v2, /device:TPU:54, one launch (start us, length us, event | category | flops | bytes accessed | tf_op | source)
XLA Modules:
  0.0 637.9 jit_solution(16248775961603585813)
XLA Ops:
  4.3 5.3 gather_fusion
  9.5 5.2 dynamic-slice_bitcast_fusion.5
  20.2 337.5 %all-reduce.1 = s32[64,64]{1,0:T(8,128)S(1)} all-reduce(s32[64,64]{1,0:T(8,128)S(1)} %reshape.306), channel_id=2, replica_groups=mesh['dp'=64,'tensor'=2] {'dp'}, use_global_device_ids=true, to_apply=%add | all-reduce | flops 4096 | bytes 32768
  359.8 2.5 broadcast_in_dim.36
  370.0 3.8 pad_maximum_fusion
  373.8 3.1 constant_dynamic-update-slice_fusion
  376.9 3.1 fusion.3
  380.0 4.7 fusion.60
  384.7 6.3 fusion.62
  391.0 8.4 %fusion.64 = f32[1024,1024]{1,0:T(8,128)} fusion(bf16[2048,1024]{1,0:T(8,128)(2,1)S(1)} %copy-done.23, bf16[1024,2048]{1,0:T(8,128)(2,1)} %constant_dynamic-update-slice_fusion, f32[2048]{0:T(1024)S(1)} %convert_element_type.94, f32[1024]{0:T(1024)S(1)} %add_rsqrt_fusion), kind=kOutput, calls=%fused_computation.148 | convolution fusion | flops 4303355904 | bytes 12595200 | tf_op jit(solution)/shard_map/dot_general | solution.py:50
  400.2 2.3 copy.44
  404.4 3.2 copy.47
  414.9 2.4 copy.34
  423.1 12.7 %collective-permute-start.20 = (bf16[4,2,4,32,128]{4,3,2,1,0:T(8,128)(2,1)}, bf16[4,2,4,32,128]{4,3,2,1,0:T(8,128)(2,1)}, u32[]{:S(2)}, u32[]{:S(2)}) collective-permute-start(bf16[4,2,4,32,128]{4,3,2,1,0:T(8,128)(2,1)} %get-tuple-element.15), channel_id=1, source_target_pairs={{0,112},{2,114},{4,116},{6,118},{8,120},{10,122},{12,124},{14,126}... | collective-permute-start | bytes 786440 | tf_op jit(solution)/shard_map/ppermute | solution.py:183
  435.9 37.0 %collective-permute-start.19 = (bf16[4,2,4,32,128]{4,3,2,1,0:T(8,128)(2,1)}, bf16[4,2,4,32,128]{4,3,2,1,0:T(8,128)(2,1)}, u32[]{:S(2)}, u32[]{:S(2)}) collective-permute-start(bf16[4,2,4,32,128]{4,3,2,1,0:T(8,128)(2,1)} %get-tuple-element.16), channel_id=1, source_target_pairs={{0,104},{2,106},{4,108},{6,110},{8,112},{10,114},{12,116},{14,118}... | collective-permute-start | bytes 786440 | tf_op jit(solution)/shard_map/ppermute | solution.py:183
  473.4 8.6 %fusion.68 = (f32[4,2,512]{2,1,0:T(2,128)S(1)}, f32[4,2,512,512]{2,3,1,0:T(8,128)}) fusion(pred[512,512]{0,1:T(8,128)(4,1)} %fusion.23, bf16[512,4,2,128]{3,0,2,1:T(8,128)(2,1)} %bitcast.189, bf16[1024,4,64]{2,0,1:T(8,128)(2,1)S(1)} %get-tuple-element.10, bf16[1024,4,64]{2,0,1:T(8,128)(2,1)S(1)} %get-tuple-element.11), kind=kOutput, calls=%fused_computation.151 | convolution fusion | flops 546308608 | bytes 10764288 | tf_op jit(solution)/shard_map/sub | solution.py:93
  482.1 4.3 fusion.20
  486.6 2.4 convolution_convert_fusion.1
  489.0 11.4 %fusion.67 = (f32[4,2,512]{2,1,0:T(2,128)S(1)}, f32[4,2,512,1024]{2,3,1,0:T(8,128)}) fusion(pred[512,1024]{0,1:T(8,128)(4,1)} %fusion.17, bf16[512,4,2,128]{3,0,2,1:T(8,128)(2,1)} %bitcast.188, bf16[1024,4,64]{2,0,1:T(8,128)(2,1)} %copy-done.10, bf16[1024,4,64]{2,0,1:T(8,128)(2,1)S(1)} %copy-done.9), kind=kOutput, calls=%fused_computation.150 | convolution fusion | flops 1092617216 | bytes 19415040 | tf_op jit(solution)/shard_map/sub | solution.py:93
  500.4 7.5 %fusion.21 = bf16[4,128,2,512]{3,1,2,0:T(8,128)(2,1)S(1)} fusion(bf16[1024,4,128,1]{0,2,3,1:T(8,128)(2,1)} %bitcast.187, f32[4,2,512,1024]{2,3,1,0:T(8,128)} %get-tuple-element.40, f32[4,2,512]{2,1,0:T(2,128)S(1)} %get-tuple-element.39), kind=kOutput, calls=%fused_computation.46 | convolution fusion | flops 1082654720 | bytes 18890752 | tf_op jit(solution)/shard_map/grqk,kgd->qgrd/dot_general | solution.py:95
  508.0 2.4 convolution_convert_fusion
  511.6 2.3 bitcast_dynamic-update-slice_fusion.15
  520.4 7.3 %collective-permute-done.9 = bf16[4,2,4,32,128]{4,3,2,1,0:T(8,128)(2,1)S(1)} collective-permute-done((bf16[4,2,4,32,128]{4,3,2,1,0:T(8,128)(2,1)S(1)}, bf16[4,2,4,32,128]{4,3,2,1,0:T(8,128)(2,1)S(1)}, u32[]{:S(2)}, u32[]{:S(2)}) %collective-permute-start.9) | collective-permute-done | bytes 262176 | tf_op jit(solution)/shard_map/ppermute | solution.py:183
  528.4 9.7 %collective-permute-done.10 = bf16[4,2,4,32,128]{4,3,2,1,0:T(8,128)(2,1)S(1)} collective-permute-done((bf16[4,2,4,32,128]{4,3,2,1,0:T(8,128)(2,1)S(1)}, bf16[4,2,4,32,128]{4,3,2,1,0:T(8,128)(2,1)S(1)}, u32[]{:S(2)}, u32[]{:S(2)}) %collective-permute-start.10) | collective-permute-done | bytes 262176 | tf_op jit(solution)/shard_map/ppermute | solution.py:183
  539.7 12.1 %collective-permute-done.12 = bf16[4,2,4,32,128]{4,3,2,1,0:T(8,128)(2,1)S(1)} collective-permute-done((bf16[4,2,4,32,128]{4,3,2,1,0:T(8,128)(2,1)S(1)}, bf16[4,2,4,32,128]{4,3,2,1,0:T(8,128)(2,1)S(1)}, u32[]{:S(2)}, u32[]{:S(2)}) %collective-permute-start.12) | collective-permute-done | bytes 262176 | tf_op jit(solution)/shard_map/ppermute | solution.py:183
  552.5 2.2 collective-permute-done.13
  555.5 11.1 %collective-permute-done.14 = bf16[4,2,4,32,128]{4,3,2,1,0:T(8,128)(2,1)S(1)} collective-permute-done((bf16[4,2,4,32,128]{4,3,2,1,0:T(8,128)(2,1)S(1)}, bf16[4,2,4,32,128]{4,3,2,1,0:T(8,128)(2,1)S(1)}, u32[]{:S(2)}, u32[]{:S(2)}) %collective-permute-start.14) | collective-permute-done | bytes 262176 | tf_op jit(solution)/shard_map/ppermute | solution.py:183
  569.6 14.2 %collective-permute-done.16 = bf16[4,2,4,32,128]{4,3,2,1,0:T(8,128)(2,1)S(1)} collective-permute-done((bf16[4,2,4,32,128]{4,3,2,1,0:T(8,128)(2,1)S(1)}, bf16[4,2,4,32,128]{4,3,2,1,0:T(8,128)(2,1)S(1)}, u32[]{:S(2)}, u32[]{:S(2)}) %collective-permute-start.16) | collective-permute-done | bytes 262176 | tf_op jit(solution)/shard_map/ppermute | solution.py:183
  584.5 2.5 collective-permute-done.17
  596.3 5.6 shard_map.122
  601.9 11.3 %collective-permute-done.5 = bf16[1024,512]{0,1:T(8,128)(2,1)S(1)} collective-permute-done((bf16[1024,512]{0,1:T(8,128)(2,1)}, bf16[1024,512]{0,1:T(8,128)(2,1)S(1)}, u32[]{:S(2)}, u32[]{:S(2)}) %collective-permute-start.5) | collective-permute-done | bytes 1048608 | tf_op jit(solution)/shard_map/ppermute | solution.py:106
  613.7 20.1 %collective-permute-done.6 = bf16[1024,512]{0,1:T(8,128)(2,1)} collective-permute-done((bf16[1024,512]{0,1:T(8,128)(2,1)}, bf16[1024,512]{0,1:T(8,128)(2,1)}, u32[]{:S(2)}, u32[]{:S(2)}) %collective-permute-start.6) | collective-permute-done | bytes 1048608 | tf_op jit(solution)/shard_map/ppermute | solution.py:106
  (155 shorter events, 62.5 us)
Async XLA Ops:
  0.6 379.3 %copy-start = (bf16[2048,512]{1,0:T(8,128)(2,1)S(1)}, bf16[2048,512]{1,0:T(8,128)(2,1)}, u32[]{:S(2)}) copy-start(bf16[2048,512]{1,0:T(8,128)(2,1)} %param.15) | copy-start | bytes 6291460
  0.6 369.1 %collective-permute-start.1 = (bf16[1024]{0:T(1024)(128)(2,1)}, bf16[1024]{0:T(1024)(128)(2,1)S(1)}, u32[]{:S(2)}, u32[]{:S(2)}) collective-permute-start(bf16[1024]{0:T(1024)(128)(2,1)} %param.12), channel_id=1, source_target_pairs={{0,1},{1,0},{2,3},{3,2},{4,5},{5,4},{6,7},{7,6},{8,9},{9,8},{10,11... | collective-permute-start | bytes 6152 | tf_op jit(solution)/shard_map/ppermute | solution.py:37
  1.6 372.2 %collective-permute-start = (bf16[1024,1024]{1,0:T(8,128)(2,1)}, bf16[1024,1024]{1,0:T(8,128)(2,1)}, u32[]{:S(2)}, u32[]{:S(2)}) collective-permute-start(bf16[1024,1024]{1,0:T(8,128)(2,1)} %param.11), channel_id=1, source_target_pairs={{0,1},{1,0},{2,3},{3,2},{4,5},{5,4},{6,7},{7,6},{8,9},{9,8},{10,11... | collective-permute-start | bytes 6291464 | tf_op jit(solution)/shard_map/ppermute | solution.py:36
  14.7 355.3 %collective-permute-start.4 = (bf16[16,2,4,32,128]{4,3,2,1,0:T(8,128)(2,1)}, bf16[16,2,4,32,128]{4,3,2,1,0:T(8,128)(2,1)}, u32[]{:S(2)}, u32[]{:S(2)}) collective-permute-start(bf16[16,2,4,32,128]{4,3,2,1,0:T(8,128)(2,1)} %get-tuple-element.32), channel_id=1, source_target_pairs={{0,6},{2,0},{4,2},{6,4},{8,14},{10,8},{12,10},{14,12},{16,22},{18,... | collective-permute-start | bytes 3145736 | tf_op jit(solution)/shard_map/ppermute | solution.py:166
  15.0 355.0 %collective-permute-start.3 = (bf16[16,2,4,32,128]{4,3,2,1,0:T(8,128)(2,1)}, bf16[16,2,4,32,128]{4,3,2,1,0:T(8,128)(2,1)}, u32[]{:S(2)}, u32[]{:S(2)}) collective-permute-start(bf16[16,2,4,32,128]{4,3,2,1,0:T(8,128)(2,1)} %get-tuple-element.33), channel_id=1, source_target_pairs={{0,4},{2,6},{4,0},{6,2},{8,12},{10,14},{12,8},{14,10},{16,20},{18,... | collective-permute-start | bytes 3145736 | tf_op jit(solution)/shard_map/ppermute | solution.py:166
  17.1 352.9 %collective-permute-start.2 = (bf16[16,2,4,32,128]{4,3,2,1,0:T(8,128)(2,1)}, bf16[16,2,4,32,128]{4,3,2,1,0:T(8,128)(2,1)}, u32[]{:S(2)}, u32[]{:S(2)}) collective-permute-start(bf16[16,2,4,32,128]{4,3,2,1,0:T(8,128)(2,1)} %get-tuple-element.34), channel_id=1, source_target_pairs={{0,2},{2,4},{4,6},{6,0},{8,10},{10,12},{12,14},{14,8},{16,18},{18,... | collective-permute-start | bytes 3145736 | tf_op jit(solution)/shard_map/ppermute | solution.py:166
  421.6 173.0 %collective-permute-start.21 = (bf16[4,2,4,32,128]{4,3,2,1,0:T(8,128)(2,1)S(1)}, bf16[4,2,4,32,128]{4,3,2,1,0:T(8,128)(2,1)}, u32[]{:S(2)}, u32[]{:S(2)}) collective-permute-start(bf16[4,2,4,32,128]{4,3,2,1,0:T(8,128)(2,1)S(1)} %get-tuple-element.14), channel_id=1, source_target_pairs={{0,120},{2,122},{4,124},{6,126},{8,0},{10,2},{12,4},{14,6},{16,8},... | collective-permute-start | bytes 786440 | tf_op jit(solution)/shard_map/ppermute | solution.py:183
  423.1 169.8 %collective-permute-start.20 = (bf16[4,2,4,32,128]{4,3,2,1,0:T(8,128)(2,1)}, bf16[4,2,4,32,128]{4,3,2,1,0:T(8,128)(2,1)}, u32[]{:S(2)}, u32[]{:S(2)}) collective-permute-start(bf16[4,2,4,32,128]{4,3,2,1,0:T(8,128)(2,1)} %get-tuple-element.15), channel_id=1, source_target_pairs={{0,112},{2,114},{4,116},{6,118},{8,120},{10,122},{12,124},{14,126}... | collective-permute-start | bytes 786440 | tf_op jit(solution)/shard_map/ppermute | solution.py:183
  435.9 155.4 %collective-permute-start.19 = (bf16[4,2,4,32,128]{4,3,2,1,0:T(8,128)(2,1)}, bf16[4,2,4,32,128]{4,3,2,1,0:T(8,128)(2,1)}, u32[]{:S(2)}, u32[]{:S(2)}) collective-permute-start(bf16[4,2,4,32,128]{4,3,2,1,0:T(8,128)(2,1)} %get-tuple-element.16), channel_id=1, source_target_pairs={{0,104},{2,106},{4,108},{6,110},{8,112},{10,114},{12,116},{14,118}... | collective-permute-start | bytes 786440 | tf_op jit(solution)/shard_map/ppermute | solution.py:183
  472.9 43.8 %collective-permute-start.8 = (bf16[4,2,4,32,128]{4,3,2,1,0:T(8,128)(2,1)}, bf16[4,2,4,32,128]{4,3,2,1,0:T(8,128)(2,1)}, u32[]{:S(2)}, u32[]{:S(2)}) collective-permute-start(bf16[4,2,4,32,128]{4,3,2,1,0:T(8,128)(2,1)} %get-tuple-element.27), channel_id=1, source_target_pairs={{0,16},{2,18},{4,20},{6,22},{8,24},{10,26},{12,28},{14,30},{16,32}... | collective-permute-start | bytes 786440 | tf_op jit(solution)/shard_map/ppermute | solution.py:183
  472.9 42.1 %collective-permute-start.7 = (bf16[4,2,4,32,128]{4,3,2,1,0:T(8,128)(2,1)}, bf16[4,2,4,32,128]{4,3,2,1,0:T(8,128)(2,1)}, u32[]{:S(2)}, u32[]{:S(2)}) collective-permute-start(bf16[4,2,4,32,128]{4,3,2,1,0:T(8,128)(2,1)} %get-tuple-element.28), channel_id=1, source_target_pairs={{0,8},{2,10},{4,12},{6,14},{8,16},{10,18},{12,20},{14,22},{16,24},... | collective-permute-start | bytes 786440 | tf_op jit(solution)/shard_map/ppermute | solution.py:183
  510.4 45.1 %copy-start.6 = (bf16[512,2048]{1,0:T(8,128)(2,1)}, bf16[512,2048]{1,0:T(8,128)(2,1)S(1)}, u32[]{:S(2)}) copy-start(bf16[512,2048]{1,0:T(8,128)(2,1)S(1)} %convolution_convert_fusion) | copy-start | bytes 6291460
  510.4 28.4 %copy-start.17 = (bf16[4,2,4,32,128]{4,3,2,1,0:T(8,128)(2,1)S(1)}, bf16[4,2,4,32,128]{4,3,2,1,0:T(8,128)(2,1)}, u32[]{:S(2)}) copy-start(bf16[4,2,4,32,128]{4,3,2,1,0:T(8,128)(2,1)} %get-tuple-element.22) | copy-start | bytes 786436
  510.4 41.4 %copy-start.16 = (bf16[4,2,4,32,128]{4,3,2,1,0:T(8,128)(2,1)S(1)}, bf16[4,2,4,32,128]{4,3,2,1,0:T(8,128)(2,1)}, u32[]{:S(2)}) copy-start(bf16[4,2,4,32,128]{4,3,2,1,0:T(8,128)(2,1)} %get-tuple-element.21) | copy-start | bytes 786436
  510.4 44.4 %copy-start.15 = (bf16[4,2,4,32,128]{4,3,2,1,0:T(8,128)(2,1)S(1)}, bf16[4,2,4,32,128]{4,3,2,1,0:T(8,128)(2,1)}, u32[]{:S(2)}) copy-start(bf16[4,2,4,32,128]{4,3,2,1,0:T(8,128)(2,1)} %get-tuple-element.20) | copy-start | bytes 786436
  510.4 56.2 %copy-start.14 = (bf16[4,2,4,32,128]{4,3,2,1,0:T(8,128)(2,1)S(1)}, bf16[4,2,4,32,128]{4,3,2,1,0:T(8,128)(2,1)}, u32[]{:S(2)}) copy-start(bf16[4,2,4,32,128]{4,3,2,1,0:T(8,128)(2,1)} %get-tuple-element.19) | copy-start | bytes 786436
  510.5 56.9 %copy-start.13 = (bf16[4,2,4,32,128]{4,3,2,1,0:T(8,128)(2,1)S(1)}, bf16[4,2,4,32,128]{4,3,2,1,0:T(8,128)(2,1)}, u32[]{:S(2)}) copy-start(bf16[4,2,4,32,128]{4,3,2,1,0:T(8,128)(2,1)} %get-tuple-element.18) | copy-start | bytes 786436
  511.6 72.2 %copy-start.12 = (bf16[4,2,4,32,128]{4,3,2,1,0:T(8,128)(2,1)S(1)}, bf16[4,2,4,32,128]{4,3,2,1,0:T(8,128)(2,1)}, u32[]{:S(2)}) copy-start(bf16[4,2,4,32,128]{4,3,2,1,0:T(8,128)(2,1)} %get-tuple-element.17) | copy-start | bytes 786436
  515.0 12.7 %collective-permute-start.9 = (bf16[4,2,4,32,128]{4,3,2,1,0:T(8,128)(2,1)S(1)}, bf16[4,2,4,32,128]{4,3,2,1,0:T(8,128)(2,1)S(1)}, u32[]{:S(2)}, u32[]{:S(2)}) collective-permute-start(bf16[4,2,4,32,128]{4,3,2,1,0:T(8,128)(2,1)S(1)} %copy-done.21), channel_id=1, source_target_pairs={{0,24},{2,26},{4,28},{6,30},{8,32},{10,34},{12,36},{14,38},{16,40}... | collective-permute-start | bytes 786440 | tf_op jit(solution)/shard_map/ppermute | solution.py:183
  516.7 21.4 %collective-permute-start.10 = (bf16[4,2,4,32,128]{4,3,2,1,0:T(8,128)(2,1)S(1)}, bf16[4,2,4,32,128]{4,3,2,1,0:T(8,128)(2,1)S(1)}, u32[]{:S(2)}, u32[]{:S(2)}) collective-permute-start(bf16[4,2,4,32,128]{4,3,2,1,0:T(8,128)(2,1)S(1)} %copy-done.20), channel_id=1, source_target_pairs={{0,32},{2,34},{4,36},{6,38},{8,40},{10,42},{12,44},{14,46},{16,48}... | collective-permute-start | bytes 786440 | tf_op jit(solution)/shard_map/ppermute | solution.py:183
  527.7 11.2 %collective-permute-start.11 = (bf16[4,2,4,32,128]{4,3,2,1,0:T(8,128)(2,1)S(1)}, bf16[4,2,4,32,128]{4,3,2,1,0:T(8,128)(2,1)S(1)}, u32[]{:S(2)}, u32[]{:S(2)}) collective-permute-start(bf16[4,2,4,32,128]{4,3,2,1,0:T(8,128)(2,1)S(1)} %copy-done.19), channel_id=1, source_target_pairs={{0,40},{2,42},{4,44},{6,46},{8,48},{10,50},{12,52},{14,54},{16,56}... | collective-permute-start | bytes 786440 | tf_op jit(solution)/shard_map/ppermute | solution.py:183
  538.1 13.7 %collective-permute-start.12 = (bf16[4,2,4,32,128]{4,3,2,1,0:T(8,128)(2,1)S(1)}, bf16[4,2,4,32,128]{4,3,2,1,0:T(8,128)(2,1)S(1)}, u32[]{:S(2)}, u32[]{:S(2)}) collective-permute-start(bf16[4,2,4,32,128]{4,3,2,1,0:T(8,128)(2,1)S(1)} %copy-done.18), channel_id=1, source_target_pairs={{0,48},{2,50},{4,52},{6,54},{8,56},{10,58},{12,60},{14,62},{16,64}... | collective-permute-start | bytes 786440 | tf_op jit(solution)/shard_map/ppermute | solution.py:183
  538.9 15.9 %collective-permute-start.13 = (bf16[4,2,4,32,128]{4,3,2,1,0:T(8,128)(2,1)S(1)}, bf16[4,2,4,32,128]{4,3,2,1,0:T(8,128)(2,1)S(1)}, u32[]{:S(2)}, u32[]{:S(2)}) collective-permute-start(bf16[4,2,4,32,128]{4,3,2,1,0:T(8,128)(2,1)S(1)} %copy-done.17), channel_id=1, source_target_pairs={{0,56},{2,58},{4,60},{6,62},{8,64},{10,66},{12,68},{14,70},{16,72}... | collective-permute-start | bytes 786440 | tf_op jit(solution)/shard_map/ppermute | solution.py:183
  551.8 14.8 %collective-permute-start.14 = (bf16[4,2,4,32,128]{4,3,2,1,0:T(8,128)(2,1)S(1)}, bf16[4,2,4,32,128]{4,3,2,1,0:T(8,128)(2,1)S(1)}, u32[]{:S(2)}, u32[]{:S(2)}) collective-permute-start(bf16[4,2,4,32,128]{4,3,2,1,0:T(8,128)(2,1)S(1)} %copy-done.16), channel_id=1, source_target_pairs={{0,64},{2,66},{4,68},{6,70},{8,72},{10,74},{12,76},{14,78},{16,80}... | collective-permute-start | bytes 786440 | tf_op jit(solution)/shard_map/ppermute | solution.py:183
  554.8 12.5 %collective-permute-start.15 = (bf16[4,2,4,32,128]{4,3,2,1,0:T(8,128)(2,1)S(1)}, bf16[4,2,4,32,128]{4,3,2,1,0:T(8,128)(2,1)S(1)}, u32[]{:S(2)}, u32[]{:S(2)}) collective-permute-start(bf16[4,2,4,32,128]{4,3,2,1,0:T(8,128)(2,1)S(1)} %copy-done.15), channel_id=1, source_target_pairs={{0,72},{2,74},{4,76},{6,78},{8,80},{10,82},{12,84},{14,86},{16,88}... | collective-permute-start | bytes 786440 | tf_op jit(solution)/shard_map/ppermute | solution.py:183
  566.6 17.2 %collective-permute-start.16 = (bf16[4,2,4,32,128]{4,3,2,1,0:T(8,128)(2,1)S(1)}, bf16[4,2,4,32,128]{4,3,2,1,0:T(8,128)(2,1)S(1)}, u32[]{:S(2)}, u32[]{:S(2)}) collective-permute-start(bf16[4,2,4,32,128]{4,3,2,1,0:T(8,128)(2,1)S(1)} %copy-done.14), channel_id=1, source_target_pairs={{0,80},{2,82},{4,84},{6,86},{8,88},{10,90},{12,92},{14,94},{16,96}... | collective-permute-start | bytes 786440 | tf_op jit(solution)/shard_map/ppermute | solution.py:183
  567.3 19.6 %collective-permute-start.17 = (bf16[4,2,4,32,128]{4,3,2,1,0:T(8,128)(2,1)S(1)}, bf16[4,2,4,32,128]{4,3,2,1,0:T(8,128)(2,1)S(1)}, u32[]{:S(2)}, u32[]{:S(2)}) collective-permute-start(bf16[4,2,4,32,128]{4,3,2,1,0:T(8,128)(2,1)S(1)} %copy-done.13), channel_id=1, source_target_pairs={{0,88},{2,90},{4,92},{6,94},{8,96},{10,98},{12,100},{14,102},{16,1... | collective-permute-start | bytes 786440 | tf_op jit(solution)/shard_map/ppermute | solution.py:183
  583.8 6.4 collective-permute-start.18
  587.0 26.3 %collective-permute-start.5 = (bf16[1024,512]{0,1:T(8,128)(2,1)}, bf16[1024,512]{0,1:T(8,128)(2,1)S(1)}, u32[]{:S(2)}, u32[]{:S(2)}) collective-permute-start(bf16[1024,512]{0,1:T(8,128)(2,1)} %dynamic-slice_bitcast_fusion.1), channel_id=1, source_target_pairs={{0,1},{1,0},{2,3},{3,2},{4,5},{5,4},{6,7},{7,6},{8,9},{9,8},{10,11... | collective-permute-start | bytes 3145736 | tf_op jit(solution)/shard_map/ppermute | solution.py:106
  590.2 43.6 %collective-permute-start.6 = (bf16[1024,512]{0,1:T(8,128)(2,1)}, bf16[1024,512]{0,1:T(8,128)(2,1)}, u32[]{:S(2)}, u32[]{:S(2)}) collective-permute-start(bf16[1024,512]{0,1:T(8,128)(2,1)} %dynamic-slice_bitcast_fusion), channel_id=1, source_target_pairs={{0,1},{1,0},{2,3},{3,2},{4,5},{5,4},{6,7},{7,6},{8,9},{9,8},{10,11... | collective-permute-start | bytes 3145736 | tf_op jit(solution)/shard_map/ppermute | solution.py:106
  601.9 31.8 %copy-start.7 = (bf16[512,2048]{1,0:T(8,128)(2,1)S(1)}, bf16[512,2048]{1,0:T(8,128)(2,1)}, u32[]{:S(2)}) copy-start(bf16[512,2048]{1,0:T(8,128)(2,1)} %copy-done.6) | copy-start | bytes 6291460
  601.9 33.6 %copy-start.4 = (bf16[1024,1024]{1,0:T(8,128)(2,1)S(1)}, bf16[1024,1024]{1,0:T(8,128)(2,1)}, u32[]{:S(2)}) copy-start(bf16[1024,1024]{1,0:T(8,128)(2,1)} %param.11) | copy-start | bytes 6291460
  (20 other events, 165.4 us)
